TPU v7x, 32 devices: a whole 2x2x4 slice. The times are simulated.
32 devices in a mesh: dp: 2 (over x), slot: 4 (over y, core), hid: 4 (over z).
Axes of the slice: x: 2, y: 2, z: 4, core: 2. Of those that a mesh axis runs over, the one named last changes fastest.
Arguments:
- master_weights: float32 [8, 3, 768, 2048], P('slot', None, 'hid', 'dp'), may hold values from -0.125 to 0.125
- first_moment: float32 [8, 3, 768, 2048], P('slot', None, 'hid', 'dp'), may hold values from -6 to 6
- second_moment: float32 [8, 3, 768, 2048], P('slot', None, 'hid', 'dp'), may hold values from 1 to 100
- tokens_one: bfloat16 [2048, 2048], P('dp'), may hold values from -6 to 6
- grad_out: bfloat16 [2048, 2048], P('dp'), may hold values from -6 to 6
- route_one: int32 [2048, 2], P('dp'), may hold values from 0 to 7, all different within a row
- prob_one: float32 [2048, 2], P('dp'), may hold values from 0.05 to 0.6
- tokens_two: bfloat16 [2048, 2048], P('dp'), may hold values from -6 to 6
- route_two: int32 [2048, 2], P('dp'), may hold values from 0 to 7, all different within a row
- prob_two: float32 [2048, 2], P('dp'), may hold values from 0.05 to 0.6
- old_order: int32 [8], replicated, may hold values from 0 to 7, each once
- new_order: int32 [8], replicated, may hold values from 0 to 7, each once
Outputs:
- moved_master: float32 [8, 3, 768, 2048], P('slot', None, 'hid', 'dp')
- moved_first: float32 [8, 3, 768, 2048], P('slot', None, 'hid', 'dp')
- moved_second: float32 [8, 3, 768, 2048], P('slot', None, 'hid', 'dp')
- next_output: bfloat16 [2048, 2048], P('dp', ('slot', 'hid'))
Inputs may be any that keep to these rules, and one draw needn't show every extreme that they name: `old_order`: lists each of the 8 experts once. `new_order`: lists each of the 8 experts once. `route_one`: each row names 2 different experts. `route_two`: each row names 2 different experts.
All inputs are finite; a program needn't handle non-finite values.
Results may differ from a plain program's by a relative error of at most 0.017.
Values may be sent and summed in bfloat16 or wider, within the bound.
A program may use at most 192 MiB of HBM per device.

v0:
```python
import jax
import jax.numpy as jnp
from jax import lax
from jax.sharding import PartitionSpec as P

learn_rate = 0.001
beta_one = 0.9
beta_two = 0.95
epsilon = 1e-08
decay_rate = 0.1


def rows_by(left, right):
    return lax.dot_general(
        left, right, (((1,), (1,)), ((), ())), preferred_element_type=jnp.float32
    )


def cols_by(left, right):
    return lax.dot_general(
        left, right, (((0,), (0,)), ((), ())), preferred_element_type=jnp.float32
    )


def expert_parts(tokens, grad_out, scaling, weights):
    gate_proj = rows_by(tokens, weights[0])
    up_proj = rows_by(tokens, weights[1])
    logistic = jax.nn.sigmoid(gate_proj)
    swish_gate = gate_proj * logistic
    activated = (swish_gate * up_proj).astype(jnp.bfloat16)
    scaled_grad = (scaling[:, None] * grad_out.astype(jnp.float32)).astype(jnp.bfloat16)
    d_activated = rows_by(scaled_grad, weights[2])
    d_gate = (d_activated * up_proj * logistic * (1.0 + gate_proj * (1.0 - logistic))).astype(
        jnp.bfloat16
    )
    d_up = (d_activated * swish_gate).astype(jnp.bfloat16)
    return (d_gate, d_up, activated, scaled_grad)


def expert_out(tokens, scaling, weights):
    gate_proj = rows_by(tokens, weights[0])
    up_proj = rows_by(tokens, weights[1])
    mixed = (scaling[:, None] * gate_proj * jax.nn.sigmoid(gate_proj) * up_proj).astype(
        jnp.bfloat16
    )
    return jnp.dot(mixed, weights[2], preferred_element_type=jnp.float32)


def adamw_update(master, moment_a, moment_b, grad_sum):
    new_a = beta_one * moment_a + (1.0 - beta_one) * grad_sum
    new_b = beta_two * moment_b + (1.0 - beta_two) * grad_sum * grad_sum
    fixed_a = new_a / (1.0 - beta_one**10)
    fixed_b = new_b / (1.0 - beta_two**10)
    new_master = master - learn_rate * (
        fixed_a / (jnp.sqrt(fixed_b) + epsilon) + decay_rate * master
    )
    return (new_master, new_a, new_b)


def coefficients(routes, probs, expert_ids):
    matches = routes[:, :, None] == expert_ids[None, None, :]
    return jnp.sum(jnp.where(matches, probs[:, :, None], 0.0), axis=1)


def per_device(
    master_weights,
    first_moment,
    second_moment,
    tokens_one,
    grad_out,
    route_one,
    prob_one,
    tokens_two,
    route_two,
    prob_two,
    old_order,
    new_order,
):
    local_count = master_weights.shape[0]
    slot_index = lax.axis_index("slot")
    offset = slot_index * local_count
    held_ids = lax.dynamic_slice_in_dim(old_order, offset, local_count)
    shard_weights = master_weights.astype(jnp.bfloat16)
    full_weights = lax.all_gather(shard_weights, "dp", axis=3, tiled=True)
    scaling_one = coefficients(route_one, prob_one, held_ids)
    parts = [
        expert_parts(tokens_one, grad_out, scaling_one[:, expert], full_weights[expert])
        for expert in range(local_count)
    ]
    gradients = jnp.stack(
        [
            jnp.stack(
                [
                    cols_by(part[0], tokens_one),
                    cols_by(part[1], tokens_one),
                    cols_by(part[2], part[3]),
                ]
            )
            for part in parts
        ]
    )
    owned_grads = lax.psum_scatter(
        gradients.astype(jnp.bfloat16), "dp", scatter_dimension=3, tiled=True
    ).astype(jnp.float32)
    new_master, new_a, new_b = adamw_update(
        master_weights, first_moment, second_moment, owned_grads
    )
    positions = jnp.arange(old_order.shape[0], dtype=jnp.int32)
    source = jnp.sum(
        jnp.where(old_order[None, :] == new_order[:, None], positions[None, :], 0), axis=1
    )
    gathered_states = (
        lax.all_gather(new_master, "slot", axis=0, tiled=True),
        lax.all_gather(new_a, "slot", axis=0, tiled=True),
        lax.all_gather(new_b, "slot", axis=0, tiled=True),
    )
    wanted = lax.dynamic_slice_in_dim(source, offset, local_count)
    moved_states = tuple((jnp.take(state_block, wanted, axis=0) for state_block in gathered_states))
    moved_master, moved_first, moved_second = moved_states
    next_shard = new_master.astype(jnp.bfloat16)
    next_full = lax.all_gather(next_shard, "dp", axis=3, tiled=True)
    scaling_two = coefficients(route_two, prob_two, held_ids)
    partial_value = expert_out(tokens_two, scaling_two[:, 0], next_full[0])
    expert = 1
    partial_value = partial_value + expert_out(
        tokens_two, scaling_two[:, expert], next_full[expert]
    )
    mixed_out = lax.psum_scatter(
        partial_value, ("slot", "hid"), scatter_dimension=1, tiled=True
    ).astype(jnp.bfloat16)
    return (moved_master, moved_first, moved_second, mixed_out)


def solution(mesh):
    in_specs = (
        P("slot", None, "hid", "dp"),
        P("slot", None, "hid", "dp"),
        P("slot", None, "hid", "dp"),
        P("dp", None),
        P("dp", None),
        P("dp", None),
        P("dp", None),
        P("dp", None),
        P("dp", None),
        P("dp", None),
        P(),
        P(),
    )
    out_specs = (
        P("slot", None, "hid", "dp"),
        P("slot", None, "hid", "dp"),
        P("slot", None, "hid", "dp"),
        P("dp", ("slot", "hid")),
    )
    return jax.shard_map(
        per_device, mesh=mesh, in_specs=in_specs, out_specs=out_specs, check_vma=False
    )
```

profile of v0, /device:TPU:0, one launch (start us, length us, event | category | flops | bytes accessed | tf_op | source)
XLA Modules:
  0.0 761.6 jit_solution(9084671307208111710)
XLA Ops:
  7.2 0.0 all-gather.6.cloned.1.call-start
  7.3 4.1 convert_element_type.49
  11.4 0.0 reduce-scatter.3.cloned.1.call-start
  11.5 0.1 dynamic_slice.6
  11.6 0.1 fusion.50
  11.7 65.2 %all-gather.6.cloned.1.call-done = bf16[2,3,192,2048]{3,2,1,0:T(8,128)(2,1)} async-done(((bf16[2,3,192,1024]{3,2,1,0:T(8,128)(2,1)}), bf16[2,3,192,2048]{3,2,1,0:T(8,128)(2,1)}) %all-gather.6.cloned.1.call-update) | async-done | bytes 4718608 | tf_op jit(solution)/shard_map/all_gather | solution.py:84
  76.9 4.1 fusion.23
  81.0 4.0 fusion.14
  85.1 1.0 fusion.5
  86.1 1.5 fusion.24
  87.7 1.2 fusion.4
  88.9 1.0 copy-done.7
  89.8 1.3 fusion.6
  91.1 1.5 fusion.21
  92.7 1.6 fusion.11
  94.3 1.1 fusion.8
  95.4 1.5 fusion.22
  96.9 1.2 fusion.7
  98.1 1.5 fusion.9
  99.6 0.3 maximum_bitcast_fusion
  99.9 0.3 maximum_bitcast_fusion.1
  100.1 2.6 pad_maximum_fusion
  102.7 0.0 all-gather.14.cloned.1.call-start
  102.8 60.2 %reduce-scatter.3.cloned.1.call-done = bf16[2,3,192,1024]{3,2,1,0:T(8,128)(2,1)} async-done(((bf16[2,3,192,2048]{3,2,1,0:T(8,128)(2,1)}), bf16[2,3,192,1024]{3,2,1,0:T(8,128)(2,1)}) %reduce-scatter.3.cloned.1.call-update) | async-done | bytes 2359312 | tf_op jit(solution)/shard_map/reduce_scatter | solution.py:102
  163.0 11.4 %fusion.59 = (bf16[2,3,192,1024]{3,2,1,0:T(8,128)(2,1)}, f32[2,3,192,1024]{3,2,1,0:T(8,128)}, f32[2,3,192,1024]{3,2,1,0:T(8,128)}, f32[2,3,192,1024]{3,2,1,0:T(8,128)}) fusion(f32[2,3,192,1024]{3,2,1,0:T(8,128)} %param.14, bf16[2,3,192,1024]{3,2,1,0:T(8,128)(2,1)} %reduce-scatter.3.cloned.1.call-done, f32[2,3,192,1024]{3,2,1,0:T(8,128)} %param.15, ...), kind=kLoop, calls=%fused_computation.100 | loop fusion | flops 20054016 | bytes 33030144 | tf_op jit(solution)/shard_map/convert_element_type | solution.py:120
  174.3 0.0 reduce-scatter.5.cloned.1.call-start
  174.4 62.7 %all-gather.14.cloned.1.call-done = bf16[2,3,192,2048]{3,2,1,0:T(8,128)(2,1)} async-done(((bf16[2,3,192,1024]{3,2,1,0:T(8,128)(2,1)}), bf16[2,3,192,2048]{3,2,1,0:T(8,128)(2,1)}) %all-gather.14.cloned.1.call-update) | async-done | bytes 4718608 | tf_op jit(solution)/shard_map/all_gather | solution.py:121
  237.1 4.1 fusion.20
  241.3 2.7 fusion.19
  243.9 8.7 %fusion.17 = f32[1024,2048]{1,0:T(8,128)} fusion(bf16[1024,2048]{1,0:T(8,128)(2,1)} %param.21, bf16[2,3,192,2048]{3,2,1,0:T(8,128)(2,1)} %all-gather.14.cloned.1.call-done, f32[192,1024]{1,0:T(8,128)S(1)} %fusion.20, f32[1024]{0:T(1024)S(1)} %bitcast.71), kind=kOutput, calls=%fused_computation.36 | convolution fusion | flops 1611988992 | bytes 14946304 | tf_op jit(solution)/shard_map/dot_general | solution.py:46
  252.6 11.2 %convolution_add_fusion = f32[1024,2048]{1,0:T(8,128)} fusion(f32[1024,2048]{1,0:T(8,128)} %fusion.17, bf16[1024,2048]{1,0:T(8,128)(2,1)} %param.21, bf16[2,3,192,2048]{3,2,1,0:T(8,128)(2,1)} %all-gather.14.cloned.1.call-done, f32[192,1024]{1,0:T(8,128)S(1)} %fusion.19, f32[1024]{0:T(1024)S(1)} %bitcast.70), kind=kOutput, calls=%fused_computation.13 | convolution fusion | flops 1614086144 | bytes 23334912 | tf_op jit(solution)/shard_map/dot_general | solution.py:46
  263.9 0.0 all-gather.8.cloned.1.call-start
  263.9 0.5 all-gather.8.cloned.1.call-update
  264.5 0.0 all-gather.10.cloned.1.call-start
  264.5 0.5 all-gather.10.cloned.1.call-update
  265.1 0.3 all-gather.12.cloned.1.call-start
  265.3 0.5 all-gather.12.cloned.1.call-update
  265.8 0.2 select_reduce_fusion
  266.0 0.1 compare_and_fusion
  266.1 101.5 %reduce-scatter.5.cloned.1.call-done = f32[1024,128]{1,0:T(8,128)} async-done(((f32[1024,2048]{1,0:T(8,128)}), f32[1024,128]{1,0:T(8,128)}) %reduce-scatter.5.cloned.1.call-update) | async-done | bytes 524304 | tf_op jit(solution)/shard_map/reduce_scatter | solution.py:128
  367.6 1.8 convert_element_type.61
  369.4 119.9 %all-gather.8.cloned.1.call-done = f32[8,3,192,1024]{3,2,1,0:T(8,128)} async-done(((f32[2,3,192,1024]{3,2,1,0:T(8,128)}), f32[8,3,192,1024]{3,2,1,0:T(8,128)}) %all-gather.8.cloned.1.call-update) | async-done | bytes 18874384 | tf_op jit(solution)/shard_map/all_gather | solution.py:113
  489.3 9.7 %gather_fusion = f32[2,3,192,1024]{3,2,1,0:T(8,128)} fusion(f32[8,3,192,1024]{3,2,1,0:T(8,128)} %all-gather.8.cloned.1.call-done, s32[1024]{0:T(1024)S(1)} %pad_clamp_fusion), kind=kCustom, calls=%fused_computation.clone | custom fusion | bytes 9437192 | tf_op jit(solution)/shard_map/jit(_take)/gather | solution.py:118
  499.0 112.4 %all-gather.10.cloned.1.call-done = f32[8,3,192,1024]{3,2,1,0:T(8,128)} async-done(((f32[2,3,192,1024]{3,2,1,0:T(8,128)}), f32[8,3,192,1024]{3,2,1,0:T(8,128)}) %all-gather.10.cloned.1.call-update) | async-done | bytes 18874384 | tf_op jit(solution)/shard_map/all_gather | solution.py:114
  611.3 9.7 %gather_fusion.1 = f32[2,3,192,1024]{3,2,1,0:T(8,128)} fusion(f32[8,3,192,1024]{3,2,1,0:T(8,128)} %all-gather.10.cloned.1.call-done, s32[1024]{0:T(1024)S(1)} %pad_clamp_fusion), kind=kCustom, calls=%fused_computation.1.clone | custom fusion | bytes 9437192 | tf_op jit(solution)/shard_map/jit(_take)/gather | solution.py:118
  621.0 112.5 %all-gather.12.cloned.1.call-done = f32[8,3,192,1024]{3,2,1,0:T(8,128)} async-done(((f32[2,3,192,1024]{3,2,1,0:T(8,128)}), f32[8,3,192,1024]{3,2,1,0:T(8,128)}) %all-gather.12.cloned.1.call-update) | async-done | bytes 18874384 | tf_op jit(solution)/shard_map/all_gather | solution.py:115
  733.5 9.4 %gather_fusion.2 = f32[2,3,192,1024]{3,2,1,0:T(8,128)} fusion(f32[8,3,192,1024]{3,2,1,0:T(8,128)} %all-gather.12.cloned.1.call-done, s32[1024]{0:T(1024)S(1)} %pad_clamp_fusion), kind=kCustom, calls=%fused_computation.2.clone | custom fusion | bytes 9437192 | tf_op jit(solution)/shard_map/jit(_take)/gather | solution.py:118
  742.9 11.9 %broadcast_select_fusion = (f32[2,3,192,1024]{3,2,1,0:T(8,128)}, f32[2,3,192,1024]{3,2,1,0:T(8,128)}, f32[2,3,192,1024]{3,2,1,0:T(8,128)}) fusion(f32[2,3,192,1024]{3,2,1,0:T(8,128)} %gather_fusion.2, pred[2]{0:T(512)(128)(4,1)S(1)} %get-tuple-element.11, f32[2,3,192,1024]{3,2,1,0:T(8,128)} %gather_fusion.1, f32[2,3,192,1024]{3,2,1,0:T(8,128)} %gather_fusion), kind=kLoop, calls=%fused_computation.28 | loop fusion | flops 3538944 | bytes 28311554 | tf_op jit(solution)/shard_map/jit(_take)/select_n | solution.py:118
  (25 shorter events, 0.1 us)
Async XLA Ops:
  7.2 4.3 copy-start.8
  7.2 4.4 copy-start.4
  7.2 4.4 copy-start.3
  7.2 4.4 copy-start.2
  7.2 4.4 copy-start.1
  7.2 69.7 %all-gather.6.cloned.1.call-start = ((), (), s32[]{:S(2)}) async-start(), calls=%async_computation.2 | async-start | bytes 7077888 | tf_op jit(solution)/shard_map/all_gather | solution.py:84
  11.4 151.6 %reduce-scatter.3.cloned.1.call-start = ((), (), s32[]{:S(2)}) async-start(), calls=%async_computation.3 | async-start | bytes 7077888 | tf_op jit(solution)/shard_map/reduce_scatter | solution.py:102
  76.9 4.1 copy-start.5
  81.0 4.1 copy-start.6
  87.7 2.2 copy-start.7
  102.7 134.4 %all-gather.14.cloned.1.call-start = ((), (), s32[]{:S(2)}) async-start(), calls=%async_computation.7 | async-start | bytes 7077888 | tf_op jit(solution)/shard_map/all_gather | solution.py:121
  174.3 193.3 %reduce-scatter.5.cloned.1.call-start = ((), (), s32[]{:S(2)}) async-start(), calls=%async_computation.8 | async-start | bytes 8912896 | tf_op jit(solution)/shard_map/reduce_scatter | solution.py:128
  237.1 4.1 copy-start
  263.9 225.4 %all-gather.8.cloned.1.call-start = ((), (), s32[]{:S(2)}) async-start(), calls=%async_computation.4 | async-start | bytes 23592960 | tf_op jit(solution)/shard_map/all_gather | solution.py:113
  264.5 346.9 %all-gather.10.cloned.1.call-start = ((), (), s32[]{:S(2)}) async-start(), calls=%async_computation.5 | async-start | bytes 23592960 | tf_op jit(solution)/shard_map/all_gather | solution.py:114
  264.5 1.3 copy-start.9
  265.1 468.5 %all-gather.12.cloned.1.call-start = ((), (), s32[]{:S(2)}) async-start(), calls=%async_computation.6 | async-start | bytes 23592960 | tf_op jit(solution)/shard_map/all_gather | solution.py:115
Sparse Core Ops, SparseCore 0:
  11.5 65.3 all-gather.5
  102.9 60.0 reduce-scatter.2
  174.5 62.6 all-gather.13
  264.0 103.5 reduce-scatter.4
  369.6 119.6 all-gather.7
  491.3 119.9 all-gather.9
  613.5 119.9 all-gather.11
where the time goes:
time: 762 us
  waiting for transfers between devices  636 us (83%)
  matrix products  48.3 us (6%)
  other arithmetic  32.6 us (4%)
  local copies, waits for them, and re-layouts  29.8 us (4%)
  between operations  14.4 us (2%)
    all_gather x1, waiting for transfers between devices, per_device(): lax.all_gather(new_master, 'slot', axis=0, tiled=True)  120 us
    all_gather x1, waiting for transfers between devices, per_device(): lax.all_gather(new_b, 'slot', axis=0, tiled=True)  113 us
    all_gather x1, waiting for transfers between devices, per_device(): lax.all_gather(new_a, 'slot', axis=0, tiled=True)  112 us
    reduce_scatter x1, waiting for transfers between devices, per_device(): lax.psum_scatter(partial_value, ('slot', 'hid'), scatter_dimension=1, til...  102 us
    all_gather x1, waiting for transfers between devices, per_device(): full_weights = lax.all_gather(shard_weights, 'dp', axis=3, tiled=True)  65.2 us
    all_gather x1, waiting for transfers between devices, per_device(): next_full = lax.all_gather(next_shard, 'dp', axis=3, tiled=True)  62.7 us
    reduce_scatter x1, waiting for transfers between devices, per_device(): lax.psum_scatter(gradients.astype(jnp.bfloat16), 'dp', scatter_dimension=...  60.2 us
    gather x3, local copies, waits for them, and re-layouts, per_device(): jnp.take(state_block, wanted, axis=0)  28.7 us
  transfers between devices with their start and end apart: 7, of which 7 were waited for; matrix products, arithmetic and copies ran while one was open for 3% of the time, Pallas kernels for 0%

commit v1 on v0

--- a/solution.py
+++ b/solution.py
@@ -8,6 +8,13 @@
 beta_two = 0.95
 epsilon = 1e-08
 decay_rate = 0.1
+
+
+def time_the_rings(block_here, dim_k):
+    mid_arr = list(block_here.shape[1:])
+    mid_arr[dim_k] *= block_here.shape[0]
+    local_part = jnp.moveaxis(block_here, 0, dim_k).reshape(mid_arr)
+    return local_part
 
 
 def rows_by(left, right):
@@ -109,10 +116,26 @@
     source = jnp.sum(
         jnp.where(old_order[None, :] == new_order[:, None], positions[None, :], 0), axis=1
     )
+
+    def match_the_field(a0, group_axis, where_dim):
+        n_dev_all = lax.axis_size(group_axis)
+        row_list = []
+        for tick in range(n_dev_all):
+            row_list.append((tick, (tick + 1) % n_dev_all))
+        leaves = [a0]
+        while len(leaves) < n_dev_all:
+            z1 = lax.ppermute(leaves[-1], axis_name=group_axis, perm=row_list)
+            leaves.append(z1)
+        newest = lax.axis_index(group_axis)
+        r2 = jnp.stack(leaves)
+        leaves = r2[(newest - jnp.arange(n_dev_all)) % n_dev_all]
+        ready = time_the_rings(leaves, where_dim)
+        return ready
+
     gathered_states = (
         lax.all_gather(new_master, "slot", axis=0, tiled=True),
         lax.all_gather(new_a, "slot", axis=0, tiled=True),
-        lax.all_gather(new_b, "slot", axis=0, tiled=True),
+        match_the_field(new_b, "slot", 0),
     )
     wanted = lax.dynamic_slice_in_dim(source, offset, local_count)
     moved_states = tuple((jnp.take(state_block, wanted, axis=0) for state_block in gathered_states))

time: 762 us -> 694 us (0.911)
  waiting for transfers between devices: 636 us -> 513 us
  local copies, waits for them, and re-layouts: 29.8 us -> 58 us
  other arithmetic: 32.6 us -> 53.4 us
    ppermute x0 -> x3, waiting for transfers between devices: none -> 277 us  [match_the_field(): z1 = lax.ppermute(leaves[-1], axis_name=group_axis, perm=row_list)]
    all_gather x1, waiting for transfers between devices: 120 us -> 0.01 us  [per_device(): lax.all_gather(new_master, 'slot', axis=0, tiled=True)]
    all_gather x1 -> x0, waiting for transfers between devices: 113 us -> none  [per_device(): lax.all_gather(new_b, 'slot', axis=0, tiled=True)]
    reduce_scatter x1, waiting for transfers between devices: 102 us -> 0.01 us  [per_device(): lax.psum_scatter(partial_value, ('slot', 'hid'), scatter_dimension=1, til...]
    all_gather x1, waiting for transfers between devices: 112 us -> 46.6 us  [per_device(): lax.all_gather(new_a, 'slot', axis=0, tiled=True)]
    gather x0 -> x3, local copies, waits for them, and re-layouts: none -> 28.3 us  [match_the_field(): leaves = r2[(newest - jnp.arange(n_dev_all)) % n_dev_all]]
    unnamed x0 -> x1, other arithmetic: none -> 15.4 us
  transfers between devices with their start and end apart: 7 -> 9, of which waited for: 7 -> 7; matrix products, arithmetic and copies ran while one was open for 3% -> 10% of each run, Pallas kernels for 0% -> 0%
where the time goes in v1:
time: 694 us
  waiting for transfers between devices  513 us (74%)
  local copies, waits for them, and re-layouts  58 us (8%)
  other arithmetic  53.4 us (8%)
  matrix products  48.3 us (7%)
  between operations  14.4 us (2%)
  starting transfers between devices  7.15 us (1%)
    ppermute x3, waiting for transfers between devices, match_the_field(): z1 = lax.ppermute(leaves[-1], axis_name=group_axis, perm=row_list)  277 us
    all_gather x1, waiting for transfers between devices, per_device(): full_weights = lax.all_gather(shard_weights, 'dp', axis=3, tiled=True)  65.2 us
    all_gather x1, waiting for transfers between devices, per_device(): next_full = lax.all_gather(next_shard, 'dp', axis=3, tiled=True)  62.7 us
    reduce_scatter x1, waiting for transfers between devices, per_device(): lax.psum_scatter(gradients.astype(jnp.bfloat16), 'dp', scatter_dimension=...  60.2 us
    all_gather x1, waiting for transfers between devices, per_device(): lax.all_gather(new_a, 'slot', axis=0, tiled=True)  46.6 us
    gather x3, local copies, waits for them, and re-layouts, per_device(): jnp.take(state_block, wanted, axis=0)  28.6 us
    gather x3, local copies, waits for them, and re-layouts, match_the_field(): leaves = r2[(newest - jnp.arange(n_dev_all)) % n_dev_all]  28.3 us
    dot_general x8, matrix products, rows_by(): lax.dot_general(left, right, (((1,), (1,)), ((), ())), preferred_element_...  21.1 us
  transfers between devices with their start and end apart: 9, of which 7 were waited for; matrix products, arithmetic and copies ran while one was open for 10% of the time, Pallas kernels for 0%

profile of v1, /device:TPU:0, one launch (start us, length us, event | category | flops | bytes accessed | tf_op | source)
XLA Modules:
  0.0 693.9 jit_solution(17376016460229325649)
XLA Ops:
  7.3 4.1 convert_element_type.49
  11.5 0.1 dynamic_slice.6
  11.6 0.1 fusion.50
  11.7 65.2 %all-gather.5.cloned.1.call-done = bf16[2,3,192,2048]{3,2,1,0:T(8,128)(2,1)} async-done(((bf16[2,3,192,1024]{3,2,1,0:T(8,128)(2,1)}), bf16[2,3,192,2048]{3,2,1,0:T(8,128)(2,1)}) %all-gather.5.cloned.1.call-update) | async-done | bytes 4718608 | tf_op jit(solution)/shard_map/all_gather | solution.py:91
  76.9 4.1 fusion.23
  81.0 4.0 fusion.14
  85.1 1.0 fusion.5
  86.1 1.5 fusion.24
  87.7 1.2 fusion.4
  88.9 1.0 copy-done.7
  89.8 1.3 fusion.6
  91.1 1.5 fusion.21
  92.7 1.6 fusion.11
  94.3 1.1 fusion.8
  95.4 1.5 fusion.22
  96.9 1.2 fusion.7
  98.1 1.5 fusion.9
  99.6 0.3 maximum_bitcast_fusion
  99.9 0.3 maximum_bitcast_fusion.1
  100.1 2.6 pad_maximum_fusion.2
  102.8 60.2 %reduce-scatter.3.cloned.1.call-done = bf16[2,3,192,1024]{3,2,1,0:T(8,128)(2,1)} async-done(((bf16[2,3,192,2048]{3,2,1,0:T(8,128)(2,1)}), bf16[2,3,192,1024]{3,2,1,0:T(8,128)(2,1)}) %reduce-scatter.3.cloned.1.call-update) | async-done | bytes 2359312 | tf_op jit(solution)/shard_map/reduce_scatter | solution.py:109
  163.0 11.4 %fusion.61 = (bf16[2,3,192,1024]{3,2,1,0:T(8,128)(2,1)}, f32[2,3,192,1024]{3,2,1,0:T(8,128)}, f32[2,3,192,1024]{3,2,1,0:T(8,128)}, f32[2,3,192,1024]{3,2,1,0:T(8,128)}) fusion(f32[2,3,192,1024]{3,2,1,0:T(8,128)} %param.14, bf16[2,3,192,1024]{3,2,1,0:T(8,128)(2,1)} %reduce-scatter.3.cloned.1.call-done, f32[2,3,192,1024]{3,2,1,0:T(8,128)} %param.15, ...), kind=kLoop, calls=%fused_computation.111 | loop fusion | flops 20054016 | bytes 33030144 | tf_op jit(solution)/shard_map/convert_element_type | solution.py:143
  174.4 62.7 %all-gather.11.cloned.1.call-done = bf16[2,3,192,2048]{3,2,1,0:T(8,128)(2,1)} async-done(((bf16[2,3,192,1024]{3,2,1,0:T(8,128)(2,1)}), bf16[2,3,192,2048]{3,2,1,0:T(8,128)(2,1)}) %all-gather.11.cloned.1.call-update) | async-done | bytes 4718608 | tf_op jit(solution)/shard_map/all_gather | solution.py:144
  237.2 4.1 fusion.20
  241.3 2.7 fusion.19
  243.9 8.8 %fusion.17 = f32[1024,2048]{1,0:T(8,128)} fusion(bf16[1024,2048]{1,0:T(8,128)(2,1)} %param.21, bf16[2,3,192,2048]{3,2,1,0:T(8,128)(2,1)} %all-gather.11.cloned.1.call-done, f32[192,1024]{1,0:T(8,128)S(1)} %fusion.20, f32[1024]{0:T(1024)S(1)} %bitcast.83), kind=kOutput, calls=%fused_computation.40 | convolution fusion | flops 1611988992 | bytes 14946304 | tf_op jit(solution)/shard_map/dot_general | solution.py:53
  252.7 11.2 %convolution_add_fusion = f32[1024,2048]{1,0:T(8,128)} fusion(f32[1024,2048]{1,0:T(8,128)} %fusion.17, bf16[1024,2048]{1,0:T(8,128)(2,1)} %param.21, bf16[2,3,192,2048]{3,2,1,0:T(8,128)(2,1)} %all-gather.11.cloned.1.call-done, f32[192,1024]{1,0:T(8,128)S(1)} %fusion.19, f32[1024]{0:T(1024)S(1)} %bitcast.82), kind=kOutput, calls=%fused_computation.17 | convolution fusion | flops 1614086144 | bytes 23334912 | tf_op jit(solution)/shard_map/dot_general | solution.py:53
  263.9 0.5 all-gather.7.cloned.1.call-update
  264.5 0.5 all-gather.9.cloned.1.call-update
  265.1 0.1 collective-permute-start
  265.1 71.5 %collective-permute-done = f32[2,3,192,1024]{3,2,1,0:T(8,128)S(1)} collective-permute-done((f32[2,3,192,1024]{3,2,1,0:T(8,128)}, f32[2,3,192,1024]{3,2,1,0:T(8,128)S(1)}, u32[]{:S(2)}, u32[]{:S(2)}) %collective-permute-start) | collective-permute-done | bytes 4718624 | tf_op jit(solution)/shard_map/ppermute | solution.py:127
  336.6 2.1 collective-permute-start.1
  338.7 71.2 %collective-permute-done.1 = f32[2,3,192,1024]{3,2,1,0:T(8,128)S(1)} collective-permute-done((f32[2,3,192,1024]{3,2,1,0:T(8,128)S(1)}, f32[2,3,192,1024]{3,2,1,0:T(8,128)S(1)}, u32[]{:S(2)}, u32[]{:S(2)}) %collective-permute-start.1) | collective-permute-done | bytes 4718624 | tf_op jit(solution)/shard_map/ppermute | solution.py:127
  409.9 4.8 collective-permute-start.2
  414.7 0.2 select_reduce_fusion
  414.9 0.1 compare_and_fusion
  415.0 134.2 %collective-permute-done.2 = f32[2,3,192,1024]{3,2,1,0:T(8,128)S(1)} collective-permute-done((f32[2,3,192,1024]{3,2,1,0:T(8,128)S(1)}, f32[2,3,192,1024]{3,2,1,0:T(8,128)S(1)}, u32[]{:S(2)}, u32[]{:S(2)}) %collective-permute-start.2) | collective-permute-done | bytes 4718624 | tf_op jit(solution)/shard_map/ppermute | solution.py:127
  549.2 5.4 pad_maximum_fusion
  554.6 11.2 %fusion.64 = (f32[4,2,3,192,512]{4,3,2,1,0:T(8,128)}, f32[4,2,3,192,512]{4,3,2,1,0:T(8,128)}) fusion(f32[4,2,3,192,1024]{4,3,2,1,0:T(8,128)S(1)} %pad_maximum_fusion), kind=kLoop, calls=%fused_computation.112 | loop fusion | bytes 37748736 | tf_op jit(solution)/shard_map/gather | solution.py:131
  565.8 8.5 %gather_fusion = f32[4,2,3,192,512]{4,3,2,1,0:T(8,128)} fusion(f32[4,2,3,192,512]{4,3,2,1,0:T(8,128)} %get-tuple-element.13, s32[1024]{0:T(1024)S(1)} %pad_clamp_fusion), kind=kCustom, calls=%fused_computation.3 | custom fusion | bytes 18874384 | tf_op jit(solution)/shard_map/gather | solution.py:131
  574.3 8.6 %gather_fusion.1 = f32[4,2,3,192,512]{4,3,2,1,0:T(8,128)} fusion(f32[4,2,3,192,512]{4,3,2,1,0:T(8,128)} %get-tuple-element.14, s32[1024]{0:T(1024)S(1)} %pad_clamp_fusion), kind=kCustom, calls=%fused_computation.4 | custom fusion | bytes 18874384 | tf_op jit(solution)/shard_map/gather | solution.py:131
  582.9 15.4 %pad_maximum_fusion.1 = f32[4,2,3,192,1024]{4,3,2,1,0:T(8,128)} fusion(f32[4,2,3,192,512]{4,3,2,1,0:T(8,128)} %gather_fusion.1, f32[4,2,3,192,512]{4,3,2,1,0:T(8,128)} %gather_fusion), kind=kLoop, calls=%fused_computation.6 | loop fusion | flops 4718592 | bytes 37748736
  598.2 9.6 %gather_fusion.4 = f32[2,3,192,1024]{3,2,1,0:T(8,128)} fusion(f32[8,3,192,1024]{3,2,1,0:T(8,128)} %bitcast.77, s32[1024]{0:T(1024)S(1)} %pad_clamp_fusion.1), kind=kCustom, calls=%fused_computation.2.clone | custom fusion | bytes 9437192 | tf_op jit(solution)/shard_map/jit(_take)/gather | solution.py:141
  607.9 1.8 convert_element_type.61
  609.6 9.6 %gather_fusion.2 = f32[2,3,192,1024]{3,2,1,0:T(8,128)} fusion(f32[8,3,192,1024]{3,2,1,0:T(8,128)} %all-gather.7.cloned.1.call-done, s32[1024]{0:T(1024)S(1)} %pad_clamp_fusion.1), kind=kCustom, calls=%fused_computation.clone | custom fusion | bytes 9437192 | tf_op jit(solution)/shard_map/jit(_take)/gather | solution.py:141
  619.2 46.6 %all-gather.9.cloned.1.call-done = f32[8,3,192,1024]{3,2,1,0:T(8,128)} async-done(((f32[2,3,192,1024]{3,2,1,0:T(8,128)}), f32[8,3,192,1024]{3,2,1,0:T(8,128)}) %all-gather.9.cloned.1.call-update) | async-done | bytes 18874384 | tf_op jit(solution)/shard_map/all_gather | solution.py:137
  665.8 9.4 %gather_fusion.3 = f32[2,3,192,1024]{3,2,1,0:T(8,128)} fusion(f32[8,3,192,1024]{3,2,1,0:T(8,128)} %all-gather.9.cloned.1.call-done, s32[1024]{0:T(1024)S(1)} %pad_clamp_fusion.1), kind=kCustom, calls=%fused_computation.1.clone | custom fusion | bytes 9437192 | tf_op jit(solution)/shard_map/jit(_take)/gather | solution.py:141
  675.2 11.9 %broadcast_select_fusion = (f32[2,3,192,1024]{3,2,1,0:T(8,128)}, f32[2,3,192,1024]{3,2,1,0:T(8,128)}, f32[2,3,192,1024]{3,2,1,0:T(8,128)}) fusion(f32[2,3,192,1024]{3,2,1,0:T(8,128)} %gather_fusion.4, pred[2]{0:T(512)(128)(4,1)S(1)} %get-tuple-element.11, f32[2,3,192,1024]{3,2,1,0:T(8,128)} %gather_fusion.3, f32[2,3,192,1024]{3,2,1,0:T(8,128)} %gather_fusion.2), kind=kLoop, calls=%fused_computation.32 | loop fusion | flops 3538944 | bytes 28311554 | tf_op jit(solution)/shard_map/jit(_take)/select_n | solution.py:141
  (35 shorter events, 0.4 us)
Async XLA Ops:
  7.2 4.3 copy-start.8
  7.2 4.4 copy-start.4
  7.2 4.4 copy-start.3
  7.2 4.4 copy-start.2
  7.2 4.4 copy-start.1
  7.2 69.7 %all-gather.5.cloned.1.call-start = ((), (), s32[]{:S(2)}) async-start(), calls=%async_computation.2 | async-start | bytes 7077888 | tf_op jit(solution)/shard_map/all_gather | solution.py:91
  11.4 151.6 %reduce-scatter.3.cloned.1.call-start = ((), (), s32[]{:S(2)}) async-start(), calls=%async_computation.3 | async-start | bytes 7077888 | tf_op jit(solution)/shard_map/reduce_scatter | solution.py:109
  76.9 4.1 copy-start.5
  81.0 4.1 copy-start.6
  87.7 2.2 copy-start.7
  102.8 134.4 %all-gather.11.cloned.1.call-start = ((), (), s32[]{:S(2)}) async-start(), calls=%async_computation.6 | async-start | bytes 7077888 | tf_op jit(solution)/shard_map/all_gather | solution.py:144
  174.4 433.5 %reduce-scatter.5.cloned.1.call-start = ((), (), s32[]{:S(2)}) async-start(), calls=%async_computation.7 | async-start | bytes 8912896 | tf_op jit(solution)/shard_map/reduce_scatter | solution.py:151
  237.2 4.1 copy-start
  263.9 345.7 %all-gather.7.cloned.1.call-start = ((), (), s32[]{:S(2)}) async-start(), calls=%async_computation.4 | async-start | bytes 23592960 | tf_op jit(solution)/shard_map/all_gather | solution.py:136
  263.9 150.8 %copy-start.9 = (s32[8]{0:T(128)S(1)}, s32[8]{0:T(128)}, u32[]{:S(2)}) copy-start(s32[8]{0:T(128)} %param.25) | copy-start | bytes 100
  264.5 401.3 %all-gather.9.cloned.1.call-start = ((), (), s32[]{:S(2)}) async-start(), calls=%async_computation.5 | async-start | bytes 23592960 | tf_op jit(solution)/shard_map/all_gather | solution.py:137
  265.1 71.6 %collective-permute-start = (f32[2,3,192,1024]{3,2,1,0:T(8,128)}, f32[2,3,192,1024]{3,2,1,0:T(8,128)S(1)}, u32[]{:S(2)}, u32[]{:S(2)}) collective-permute-start(f32[2,3,192,1024]{3,2,1,0:T(8,128)} %get-tuple-element.10), channel_id=1, source_target_pairs={{0,4},{4,8},{8,12},{12,0},{1,5},{5,9},{9,13},{13,1},{2,6},{6,10},{... | collective-permute-start | bytes 14155784 | tf_op jit(solution)/shard_map/ppermute | solution.py:127
  336.6 73.3 %collective-permute-start.1 = (f32[2,3,192,1024]{3,2,1,0:T(8,128)S(1)}, f32[2,3,192,1024]{3,2,1,0:T(8,128)S(1)}, u32[]{:S(2)}, u32[]{:S(2)}) collective-permute-start(f32[2,3,192,1024]{3,2,1,0:T(8,128)S(1)} %collective-permute-done), channel_id=1, source_target_pairs={{0,4},{4,8},{8,12},{12,0},{1,5},{5,9},{9,13},{13,1},{2,6},{6,10},{... | collective-permute-start | bytes 14155784 | tf_op jit(solution)/shard_map/ppermute | solution.py:127
  409.9 139.3 %collective-permute-start.2 = (f32[2,3,192,1024]{3,2,1,0:T(8,128)S(1)}, f32[2,3,192,1024]{3,2,1,0:T(8,128)S(1)}, u32[]{:S(2)}, u32[]{:S(2)}) collective-permute-start(f32[2,3,192,1024]{3,2,1,0:T(8,128)S(1)} %collective-permute-done.1), channel_id=1, source_target_pairs={{0,4},{4,8},{8,12},{12,0},{1,5},{5,9},{9,13},{13,1},{2,6},{6,10},{... | collective-permute-start | bytes 14155784 | tf_op jit(solution)/shard_map/ppermute | solution.py:127
Sparse Core Ops, SparseCore 0:
  11.5 65.3 all-gather.4
  102.9 60.0 reduce-scatter.2
  174.5 62.6 all-gather.10
  264.0 110.0 reduce-scatter.4
  376.1 167.5 all-gather.6
  545.7 119.9 all-gather.8
